TPU v7x, 512 devices: a whole 4x8x8 slice. The times are simulated.
512 devices in a mesh: dp: 64 (over z_lo, y, core), mp: 8 (over x, z_hi).
Axes of the slice: x: 4, y: 8, z: 8 (z_hi: 2, z_lo: 4; z = z_hi * 4 + z_lo), core: 2. Of those that a mesh axis runs over, the one named last changes fastest.
Arguments:
- activations: bfloat16 [65536, 4096], P('dp', 'mp'), may hold values from -6 to 6
- out_grad: bfloat16 [65536, 14336], P('dp', 'mp'), may hold values from -0.0234375 to 0.0234375
- tile_list: int32 [8, 64, 2], P('mp'), may hold values from 0 to 111, as said below
- tile_count: int32 [8], P('mp'), may hold values from 32 to 64, as said below
Outputs:
- grad_tiles: float32 [8, 64, 128, 128], P('mp', 'dp')
Inputs may be any that keep to these rules, and one draw needn't show every extreme that they name: `tile_list`: in shard c the 64 entries name distinct blocks; the block row lies in 0 to 31 and the block column in c * 14 to (c + 1) * 14 - 1. `tile_count`: some shard has all 64 slots live.
All inputs are finite; a program needn't handle non-finite values.
Results may differ from a plain program's by a relative error of at most 0.0003.
Values may be sent and summed in bfloat16 or wider, within the bound.
A program may use at most 128 MiB of HBM per device.

v0:
```python
import math
import jax
import jax.numpy as jnp
from jax import lax
from jax.sharding import PartitionSpec as P

D = 4096
BLK = 128


def on_device(activations, out_grad, tile_list, tile_count):
    gathered = lax.all_gather(activations, "mp", axis=1, tiled=True)
    token_count = gathered.shape[0]
    slot_total = tile_list.shape[1]
    col_blocks = out_grad.shape[1] // BLK
    row_ids = tile_list[0, :, 0]
    col_ids = tile_list[0, :, 1] - lax.axis_index("mp") * col_blocks
    active = (jnp.arange(slot_total, dtype=jnp.int32) < tile_count[0]).astype(jnp.float32)
    act_blocks = gathered.reshape(token_count, D // BLK, BLK)
    grad_blocks = out_grad.reshape(token_count, col_blocks, BLK)

    def group_product(indices):
        act_sel = jnp.take(act_blocks, indices[0], axis=1)
        grad_sel = jnp.take(grad_blocks, indices[1], axis=1)
        return jnp.einsum("tkr,tkc->krc", act_sel, grad_sel, preferred_element_type=jnp.float32)

    count = row_ids.shape[0]
    group_size = math.gcd(count, 16)
    result = lax.map(
        group_product, (row_ids.reshape(-1, group_size), col_ids.reshape(-1, group_size))
    )
    summed = lax.psum_scatter(
        result.reshape(count, BLK, BLK) * active[:, None, None],
        "dp",
        scatter_dimension=0,
        tiled=True,
    )
    return summed[None]


def solution(mesh):
    placed = (P("dp", "mp"), P("dp", "mp"), P("mp", None, None), P("mp"))
    return jax.shard_map(
        on_device, mesh=mesh, in_specs=placed, out_specs=P("mp", "dp", None, None), check_vma=False
    )
```

profile of v0, /device:TPU:2, one launch (start us, length us, event | category | flops | bytes accessed | tf_op | source)
XLA Modules:
  0.0 573.7 jit_solution(4600374275060258306)
XLA Ops:
  6.5 0.0 all-gather.2.cloned.1.call-start
  6.5 2.3 copy.11
  8.8 0.0 all-gather.2.cloned.1.call-update
  8.8 0.0 reduce-scatter.2.cloned.1.call-start
  8.9 0.8 subtract_reduce_fusion
  9.7 0.1 reshape_squeeze.3
  9.8 0.1 sub.12
  9.8 5.9 %copy.12 = bf16[1024,1792]{0,1:T(8,128)(2,1)} copy(bf16[1024,1792]{1,0:T(8,128)(2,1)} %param.7) | data formatting | bytes 7340032 | tf_op args[1]
  15.8 5.9 %copy.14 = bf16[1024,14,128]{2,0,1:T(8,128)(2,1)} copy(bf16[1024,14,128]{0,2,1:T(8,128)(2,1)} %bitcast.49) | data formatting | bytes 7340032 | tf_op jit(solution)/shard_map/while | solution.py:29
  22.3 171.0 %all-gather.2.cloned.1.call-done = bf16[1024,4096]{0,1:T(8,128)(2,1)} async-done(((bf16[1024,512]{0,1:T(8,128)(2,1)}), bf16[1024,4096]{0,1:T(8,128)(2,1)}) %all-gather.2.cloned.1.call-update) | async-done | bytes 8388624 | tf_op jit(solution)/shard_map/all_gather | solution.py:12
  193.3 11.9 %copy.13 = bf16[1024,32,128]{2,0,1:T(8,128)(2,1)} copy(bf16[1024,32,128]{0,2,1:T(8,128)(2,1)} %bitcast.50) | data formatting | bytes 16777216 | tf_op jit(solution)/shard_map/while | solution.py:29
  205.3 70.6 %while.10 = (s32[]{:T(128)}, f32[4,16,128,128]{3,2,1,0:T(8,128)}, s32[4,16]{1,0:T(4,128)S(1)}, bf16[1024,32,128]{2,0,1:T(8,128)(2,1)}, s32[4,16]{1,0:T(4,128)S(1)}, /*index=5*/bf16[1024,14,128]{2,0,1:T(8,128)(2,1)}, s32[]{:T(128)}) while((s32[]{:T(128)}, f32[4,16,128,128]{3,2,1,0:T(8,128)}, s32[4,16]{1,0:T(4,128)S(1)}, ...), condition=%wide.region_1.2_spmd, body=%wide.region_0.1_spmd.sunk | while | flops 541067584 | bytes 26223892 | solution.py:29
  205.3 5.1 gather_fusion
  210.4 6.4 %gather_fusion.1 = bf16[16,1024,128]{2,1,0:T(8,128)(2,1)} fusion(bf16[1024,32,128]{2,0,1:T(8,128)(2,1)} %get-tuple-element.130, s32[1024]{0:T(1024)S(1)} %pad_clamp_fusion.5), kind=kCustom, calls=%fused_computation.clone.1 | custom fusion | bytes 8388672 | tf_op jit(solution)/shard_map/while/body/eval_jaxpr/jit(_take)/gather | solution.py:23
  216.8 6.1 %fusion.28 = f32[4,16,128,128]{3,2,1,0:T(8,128)} fusion(f32[4,16,128,128]{3,2,1,0:T(8,128)} %get-tuple-element.121, s32[]{:T(128)} %get-tuple-element.120, bf16[16,1024,128]{2,1,0:T(8,128)(2,1)} %gather_fusion, pred[16]{0:T(512)(128)(4,1)S(1)} %get-tuple-element.110, bf16[16,1024,128]{2,1,0:T(8,128)(2,1)} %gather_fusion.1, ...), kind=kOutput, calls=%fused_computation.11.clone.1 | convolution fusion | flops 541065216 | bytes 9437728 | tf_op jit(solution)/shard_map/while/body/eval_jaxpr/tkr,tkc->krc/dot_general | solution.py:25
  222.9 5.1 gather_fusion
  228.0 6.4 %gather_fusion.1 = bf16[16,1024,128]{2,1,0:T(8,128)(2,1)} fusion(bf16[1024,32,128]{2,0,1:T(8,128)(2,1)} %get-tuple-element.130, s32[1024]{0:T(1024)S(1)} %pad_clamp_fusion.5), kind=kCustom, calls=%fused_computation.clone.1 | custom fusion | bytes 8388672 | tf_op jit(solution)/shard_map/while/body/eval_jaxpr/jit(_take)/gather | solution.py:23
  234.4 6.1 %fusion.28 = f32[4,16,128,128]{3,2,1,0:T(8,128)} fusion(f32[4,16,128,128]{3,2,1,0:T(8,128)} %get-tuple-element.121, s32[]{:T(128)} %get-tuple-element.120, bf16[16,1024,128]{2,1,0:T(8,128)(2,1)} %gather_fusion, pred[16]{0:T(512)(128)(4,1)S(1)} %get-tuple-element.110, bf16[16,1024,128]{2,1,0:T(8,128)(2,1)} %gather_fusion.1, ...), kind=kOutput, calls=%fused_computation.11.clone.1 | convolution fusion | flops 541065216 | bytes 9437728 | tf_op jit(solution)/shard_map/while/body/eval_jaxpr/tkr,tkc->krc/dot_general | solution.py:25
  240.6 5.1 gather_fusion
  245.7 6.4 %gather_fusion.1 = bf16[16,1024,128]{2,1,0:T(8,128)(2,1)} fusion(bf16[1024,32,128]{2,0,1:T(8,128)(2,1)} %get-tuple-element.130, s32[1024]{0:T(1024)S(1)} %pad_clamp_fusion.5), kind=kCustom, calls=%fused_computation.clone.1 | custom fusion | bytes 8388672 | tf_op jit(solution)/shard_map/while/body/eval_jaxpr/jit(_take)/gather | solution.py:23
  252.1 6.1 %fusion.28 = f32[4,16,128,128]{3,2,1,0:T(8,128)} fusion(f32[4,16,128,128]{3,2,1,0:T(8,128)} %get-tuple-element.121, s32[]{:T(128)} %get-tuple-element.120, bf16[16,1024,128]{2,1,0:T(8,128)(2,1)} %gather_fusion, pred[16]{0:T(512)(128)(4,1)S(1)} %get-tuple-element.110, bf16[16,1024,128]{2,1,0:T(8,128)(2,1)} %gather_fusion.1, ...), kind=kOutput, calls=%fused_computation.11.clone.1 | convolution fusion | flops 541065216 | bytes 9437728 | tf_op jit(solution)/shard_map/while/body/eval_jaxpr/tkr,tkc->krc/dot_general | solution.py:25
  258.2 5.1 gather_fusion
  263.3 6.4 %gather_fusion.1 = bf16[16,1024,128]{2,1,0:T(8,128)(2,1)} fusion(bf16[1024,32,128]{2,0,1:T(8,128)(2,1)} %get-tuple-element.130, s32[1024]{0:T(1024)S(1)} %pad_clamp_fusion.5), kind=kCustom, calls=%fused_computation.clone.1 | custom fusion | bytes 8388672 | tf_op jit(solution)/shard_map/while/body/eval_jaxpr/jit(_take)/gather | solution.py:23
  269.7 6.1 %fusion.28 = f32[4,16,128,128]{3,2,1,0:T(8,128)} fusion(f32[4,16,128,128]{3,2,1,0:T(8,128)} %get-tuple-element.121, s32[]{:T(128)} %get-tuple-element.120, bf16[16,1024,128]{2,1,0:T(8,128)(2,1)} %gather_fusion, pred[16]{0:T(512)(128)(4,1)S(1)} %get-tuple-element.110, bf16[16,1024,128]{2,1,0:T(8,128)(2,1)} %gather_fusion.1, ...), kind=kOutput, calls=%fused_computation.11.clone.1 | convolution fusion | flops 541065216 | bytes 9437728 | tf_op jit(solution)/shard_map/while/body/eval_jaxpr/tkr,tkc->krc/dot_general | solution.py:25
  275.8 4.5 bitcast_multiply_fusion
  280.3 0.0 reduce-scatter.2.cloned.1.call-update
  280.3 286.6 %reduce-scatter.2.cloned.1.call-done = f32[1,128,128]{2,1,0:T(8,128)} async-done(((f32[64,128,128]{2,1,0:T(8,128)}), f32[1,128,128]{2,1,0:T(8,128)}) %reduce-scatter.2.cloned.1.call-update) | async-done | bytes 65552 | tf_op jit(solution)/shard_map/reduce_scatter | solution.py:32
  (18 shorter events, 0.1 us)
Async XLA Ops:
  6.5 186.8 %all-gather.2.cloned.1.call-start = ((), (), s32[]{:S(2)}) async-start(), calls=%async_computation.1 | async-start | bytes 9437184 | tf_op jit(solution)/shard_map/all_gather | solution.py:12
  8.8 558.0 %reduce-scatter.2.cloned.1.call-start = ((), (), s32[]{:S(2)}) async-start(), calls=%async_computation.2 | async-start | bytes 4259840 | tf_op jit(solution)/shard_map/reduce_scatter | solution.py:32
Sparse Core Ops, SparseCore 0:
  10.5 182.7 all-gather.1
  280.4 286.3 reduce-scatter.1
where the time goes:
time: 575 us; the launch traced here: 574 us
  waiting for transfers between devices  458 us (80%)
  local copies, waits for them, and re-layouts  72.2 us (13%)
  matrix products  24.5 us (4%)
  between operations  14.1 us (2%)
    reduce_scatter x1, waiting for transfers between devices, on_device(): lax.psum_scatter(result.reshape(count, BLK, BLK) * active[:, None, None],...  287 us
    all_gather x1, waiting for transfers between devices, on_device(): gathered = lax.all_gather(activations, 'mp', axis=1, tiled=True)  171 us
    gather x4, local copies, waits for them, and re-layouts, group_product(): act_sel = jnp.take(act_blocks, indices[0], axis=1)  25.6 us
    dot_general x4, matrix products, group_product(): jnp.einsum('tkr,tkc->krc', act_sel, grad_sel, preferred_element_type=jnp....  24.5 us
    gather x4, local copies, waits for them, and re-layouts, group_product(): grad_sel = jnp.take(grad_blocks, indices[1], axis=1)  20.3 us
    while x2, local copies, waits for them, and re-layouts, on_device(): lax.map(group_product, (row_ids.reshape(-1, group_size), col_ids.reshape(...  17.8 us
  transfers between devices with their start and end apart: 2, of which 2 were waited for; matrix products, arithmetic and copies ran while one was open for 2% of the time, Pallas kernels for 0%

commit v1 on v0

--- a/solution.py
+++ b/solution.py
@@ -9,7 +9,8 @@
 
 
 def on_device(activations, out_grad, tile_list, tile_count):
-    gathered = lax.all_gather(activations, "mp", axis=1, tiled=True)
+    outgoing = jnp.stack([activations] * lax.axis_size("mp"))
+    gathered = jnp.concatenate(lax.all_to_all(outgoing, "mp", 0, 0), axis=1)
     token_count = gathered.shape[0]
     slot_total = tile_list.shape[1]
     col_blocks = out_grad.shape[1] // BLK

time: 575 us -> 605 us (1.052)
  waiting for transfers between devices: 458 us -> 472 us
  starting transfers between devices: 0.04 us -> 13.4 us
    all_to_all x0 -> x1, waiting for transfers between devices: none -> 174 us  [on_device(): gathered = jnp.concatenate(lax.all_to_all(outgoing, 'mp', 0, 0), axis=1)]
    all_gather x1 -> x0, waiting for transfers between devices: 171 us -> none  [on_device(): gathered = lax.all_gather(activations, 'mp', axis=1, tiled=True)]
    all_to_all x0 -> x1, starting transfers between devices: none -> 13.4 us  [on_device(): gathered = jnp.concatenate(lax.all_to_all(outgoing, 'mp', 0, 0), axis=1)]
    reduce_scatter x1, waiting for transfers between devices: 287 us -> 297 us  [on_device(): lax.psum_scatter(result.reshape(count, BLK, BLK) * active[:, None, None],...]
where the time goes in v1:
time: 605 us; the launch traced here: 604 us
  waiting for transfers between devices  472 us (78%)
  local copies, waits for them, and re-layouts  75.6 us (12%)
  matrix products  24.5 us (4%)
  between operations  14.1 us (2%)
  starting transfers between devices  13.4 us (2%)
    reduce_scatter x1, waiting for transfers between devices, on_device(): lax.psum_scatter(result.reshape(count, BLK, BLK) * active[:, None, None],...  297 us
    all_to_all x1, waiting for transfers between devices, on_device(): gathered = jnp.concatenate(lax.all_to_all(outgoing, 'mp', 0, 0), axis=1)  174 us
    gather x4, local copies, waits for them, and re-layouts, group_product(): act_sel = jnp.take(act_blocks, indices[0], axis=1)  25.6 us
    dot_general x4, matrix products, group_product(): jnp.einsum('tkr,tkc->krc', act_sel, grad_sel, preferred_element_type=jnp....  24.5 us
    gather x4, local copies, waits for them, and re-layouts, group_product(): grad_sel = jnp.take(grad_blocks, indices[1], axis=1)  20.3 us
    while x2, local copies, waits for them, and re-layouts, on_device(): lax.map(group_product, (row_ids.reshape(-1, group_size), col_ids.reshape(...  17.8 us
    all_to_all x1, starting transfers between devices, on_device(): gathered = jnp.concatenate(lax.all_to_all(outgoing, 'mp', 0, 0), axis=1)  13.4 us
  transfers between devices with their start and end apart: 2, of which 2 were waited for; matrix products, arithmetic and copies ran while one was open for 2% of the time, Pallas kernels for 0%

profile of v1, /device:TPU:2, one launch (start us, length us, event | category | flops | bytes accessed | tf_op | source)
XLA Modules:
  0.0 603.8 jit_solution(13250337778743615635)
XLA Ops:
  6.5 1.5 copy.11
  8.0 4.3 stack.2
  12.3 0.0 copy-start
  12.3 13.4 %all-to-all-start = ((bf16[8,1024,512]{1,2,0:T(8,128)(2,1)}), bf16[8,1024,512]{1,2,0:T(8,128)(2,1)}, u32[]{:S(2)}, u32[]{:S(2)}) async-start(bf16[8,1024,512]{1,2,0:T(8,128)(2,1)} %stack.2), calls=%async_computation | async-start | bytes 16777216 | tf_op jit(solution)/shard_map/all_to_all | solution.py:13
  25.7 0.0 reduce-scatter.2.cloned.1.call-start
  25.7 0.0 copy-done
  25.8 0.1 reshape_squeeze.3
  25.8 0.1 sub.12
  25.9 5.9 copy.12
  31.8 5.9 copy.14
  38.4 174.1 %all-to-all-done = bf16[8,1024,512]{1,2,0:T(8,128)(2,1)} async-done(((bf16[8,1024,512]{1,2,0:T(8,128)(2,1)}), bf16[8,1024,512]{1,2,0:T(8,128)(2,1)}, u32[]{:S(2)}, u32[]{:S(2)}) %all-to-all-start) | async-done | bytes 8388640 | tf_op jit(solution)/shard_map/all_to_all | solution.py:13
  212.5 11.9 %copy.13 = bf16[1024,32,128]{2,0,1:T(8,128)(2,1)} copy(bf16[1024,32,128]{0,2,1:T(8,128)(2,1)} %bitcast.10) | data formatting | bytes 16777216 | tf_op jit(solution)/shard_map/while | solution.py:30
  224.4 70.6 %while.10 = (s32[]{:T(128)}, f32[4,16,128,128]{3,2,1,0:T(8,128)}, s32[4,16]{1,0:T(4,128)S(1)}, bf16[1024,32,128]{2,0,1:T(8,128)(2,1)}, s32[4,16]{1,0:T(4,128)S(1)}, /*index=5*/bf16[1024,14,128]{2,0,1:T(8,128)(2,1)}, s32[]{:T(128)}) while((s32[]{:T(128)}, f32[4,16,128,128]{3,2,1,0:T(8,128)}, s32[4,16]{1,0:T(4,128)S(1)}, ...), condition=%wide.region_1.2_spmd, body=%wide.region_0.1_spmd.sunk | while | flops 541067584 | bytes 26223892 | solution.py:30
  224.5 5.1 gather_fusion
  229.5 6.4 %gather_fusion.1 = bf16[16,1024,128]{2,1,0:T(8,128)(2,1)} fusion(bf16[1024,32,128]{2,0,1:T(8,128)(2,1)} %get-tuple-element.130, s32[1024]{0:T(1024)S(1)} %pad_clamp_fusion.5), kind=kCustom, calls=%fused_computation.clone.1 | custom fusion | bytes 8388672 | tf_op jit(solution)/shard_map/while/body/eval_jaxpr/jit(_take)/gather | solution.py:24
  236.0 6.1 %fusion.28 = f32[4,16,128,128]{3,2,1,0:T(8,128)} fusion(f32[4,16,128,128]{3,2,1,0:T(8,128)} %get-tuple-element.121, s32[]{:T(128)} %get-tuple-element.120, bf16[16,1024,128]{2,1,0:T(8,128)(2,1)} %gather_fusion, pred[16]{0:T(512)(128)(4,1)S(1)} %get-tuple-element.110, bf16[16,1024,128]{2,1,0:T(8,128)(2,1)} %gather_fusion.1, ...), kind=kOutput, calls=%fused_computation.11.clone.1 | convolution fusion | flops 541065216 | bytes 9437728 | tf_op jit(solution)/shard_map/while/body/eval_jaxpr/tkr,tkc->krc/dot_general | solution.py:26
  242.1 5.1 gather_fusion
  247.2 6.4 %gather_fusion.1 = bf16[16,1024,128]{2,1,0:T(8,128)(2,1)} fusion(bf16[1024,32,128]{2,0,1:T(8,128)(2,1)} %get-tuple-element.130, s32[1024]{0:T(1024)S(1)} %pad_clamp_fusion.5), kind=kCustom, calls=%fused_computation.clone.1 | custom fusion | bytes 8388672 | tf_op jit(solution)/shard_map/while/body/eval_jaxpr/jit(_take)/gather | solution.py:24
  253.6 6.1 %fusion.28 = f32[4,16,128,128]{3,2,1,0:T(8,128)} fusion(f32[4,16,128,128]{3,2,1,0:T(8,128)} %get-tuple-element.121, s32[]{:T(128)} %get-tuple-element.120, bf16[16,1024,128]{2,1,0:T(8,128)(2,1)} %gather_fusion, pred[16]{0:T(512)(128)(4,1)S(1)} %get-tuple-element.110, bf16[16,1024,128]{2,1,0:T(8,128)(2,1)} %gather_fusion.1, ...), kind=kOutput, calls=%fused_computation.11.clone.1 | convolution fusion | flops 541065216 | bytes 9437728 | tf_op jit(solution)/shard_map/while/body/eval_jaxpr/tkr,tkc->krc/dot_general | solution.py:26
  259.8 5.1 gather_fusion
  264.8 6.4 %gather_fusion.1 = bf16[16,1024,128]{2,1,0:T(8,128)(2,1)} fusion(bf16[1024,32,128]{2,0,1:T(8,128)(2,1)} %get-tuple-element.130, s32[1024]{0:T(1024)S(1)} %pad_clamp_fusion.5), kind=kCustom, calls=%fused_computation.clone.1 | custom fusion | bytes 8388672 | tf_op jit(solution)/shard_map/while/body/eval_jaxpr/jit(_take)/gather | solution.py:24
  271.3 6.1 %fusion.28 = f32[4,16,128,128]{3,2,1,0:T(8,128)} fusion(f32[4,16,128,128]{3,2,1,0:T(8,128)} %get-tuple-element.121, s32[]{:T(128)} %get-tuple-element.120, bf16[16,1024,128]{2,1,0:T(8,128)(2,1)} %gather_fusion, pred[16]{0:T(512)(128)(4,1)S(1)} %get-tuple-element.110, bf16[16,1024,128]{2,1,0:T(8,128)(2,1)} %gather_fusion.1, ...), kind=kOutput, calls=%fused_computation.11.clone.1 | convolution fusion | flops 541065216 | bytes 9437728 | tf_op jit(solution)/shard_map/while/body/eval_jaxpr/tkr,tkc->krc/dot_general | solution.py:26
  277.4 5.1 gather_fusion
  282.5 6.4 %gather_fusion.1 = bf16[16,1024,128]{2,1,0:T(8,128)(2,1)} fusion(bf16[1024,32,128]{2,0,1:T(8,128)(2,1)} %get-tuple-element.130, s32[1024]{0:T(1024)S(1)} %pad_clamp_fusion.5), kind=kCustom, calls=%fused_computation.clone.1 | custom fusion | bytes 8388672 | tf_op jit(solution)/shard_map/while/body/eval_jaxpr/jit(_take)/gather | solution.py:24
  288.9 6.1 %fusion.28 = f32[4,16,128,128]{3,2,1,0:T(8,128)} fusion(f32[4,16,128,128]{3,2,1,0:T(8,128)} %get-tuple-element.121, s32[]{:T(128)} %get-tuple-element.120, bf16[16,1024,128]{2,1,0:T(8,128)(2,1)} %gather_fusion, pred[16]{0:T(512)(128)(4,1)S(1)} %get-tuple-element.110, bf16[16,1024,128]{2,1,0:T(8,128)(2,1)} %gather_fusion.1, ...), kind=kOutput, calls=%fused_computation.11.clone.1 | convolution fusion | flops 541065216 | bytes 9437728 | tf_op jit(solution)/shard_map/while/body/eval_jaxpr/tkr,tkc->krc/dot_general | solution.py:26
  295.0 4.5 bitcast_multiply_fusion
  299.5 0.0 reduce-scatter.2.cloned.1.call-update
  299.5 297.5 %reduce-scatter.2.cloned.1.call-done = f32[1,128,128]{2,1,0:T(8,128)} async-done(((f32[64,128,128]{2,1,0:T(8,128)}), f32[1,128,128]{2,1,0:T(8,128)}) %reduce-scatter.2.cloned.1.call-update) | async-done | bytes 65552 | tf_op jit(solution)/shard_map/reduce_scatter | solution.py:33
  (19 shorter events, 0.1 us)
Async XLA Ops:
  12.3 13.4 %copy-start = (s32[1,64,2]{1,2,0:T(2,128)S(1)}, s32[1,64,2]{1,2,0:T(2,128)}, u32[]{:S(2)}) copy-start(s32[1,64,2]{1,2,0:T(2,128)} %param.8) | copy-start | bytes 1540
  12.3 200.2 %all-to-all-start = ((bf16[8,1024,512]{1,2,0:T(8,128)(2,1)}), bf16[8,1024,512]{1,2,0:T(8,128)(2,1)}, u32[]{:S(2)}, u32[]{:S(2)}) async-start(bf16[8,1024,512]{1,2,0:T(8,128)(2,1)} %stack.2), calls=%async_computation | async-start | bytes 16777216 | tf_op jit(solution)/shard_map/all_to_all | solution.py:13
  25.7 571.2 %reduce-scatter.2.cloned.1.call-start = ((), (), s32[]{:S(2)}) async-start(), calls=%async_computation.2 | async-start | bytes 4259840 | tf_op jit(solution)/shard_map/reduce_scatter | solution.py:33
Sparse Core Ops, SparseCore 0:
  299.6 297.2 reduce-scatter.1
